TPU v7x, 256 devices: a whole 4x4x8 slice. The times are simulated.
256 devices in a mesh: head: 4 (over x), page: 64 (over y, z, core).
Axes of the slice: x: 4, y: 4, z: 8, core: 2. Of those that a mesh axis runs over, the one named last changes fastest.
Arguments:
- hidden: bfloat16 [12, 2048], P(None, 'page'), may hold values from -6 to 6
- q_weight: bfloat16 [2048, 3072], P('page', 'head'), may hold values from -0.125 to 0.125
- key_up: bfloat16 [16, 128, 512], P('head'), may hold values from -0.5 to 0.5
- value_up_weight: bfloat16 [16, 512, 128], P('head'), may hold values from -0.25 to 0.25
- out_weight: bfloat16 [2048, 2048], P('head', 'page'), may hold values from -0.125 to 0.125
- cache: bfloat16 [16, 512, 128, 576], P('head', 'page'), may hold values from -360 to 360
- page_table: int32 [16, 512], P('head', 'page'), may hold values from 0 to 511, each once within a row
- seq_pages: int32 [12], replicated, may hold values from 1 to 128, 512 in all
- keep_rows: int32 [16, 512, 64], P('head'), may hold values from 0 to 127, as said below
- fold_mass: bfloat16 [16, 512, 64], P('head'), may hold values from 0.5 to 4
- new_place: int32 [16, 512], P('head'), may hold values from 0 to 2047, as said below
- norm_gain: bfloat16 [2048], replicated, may hold values from 0.099609375 to 1.8984375
- router: bfloat16 [2048, 64], replicated, may hold values from -0.125 to 0.125
- routes: int32 [12, 6], replicated, may hold values from 0 to 63, all different within a row
- w_gate: bfloat16 [64, 2048, 1408], P('page', None, 'head'), may hold values from -0.125 to 0.125
- w_up: bfloat16 [64, 2048, 1408], P('page', None, 'head'), may hold values from -0.125 to 0.125
- w_down: bfloat16 [64, 1408, 2048], P('page', 'head'), may hold values from -0.15625 to 0.15625
Outputs:
- attn_out: bfloat16 [12, 2048], replicated
- moe_out: bfloat16 [12, 2048], replicated
- new_rows: bfloat16 [8192, 64, 576], P(('head', 'page'))
- new_mass: bfloat16 [8192, 64], P(('head', 'page'))
Inputs may be any that keep to these rules, and one draw needn't show every extreme that they name: `keep_rows`: the 64 entries of each head and page are distinct. `new_place`: for each group of heads h // 4 the places form a permutation of 0 to 2047. Among the blocks of one head group whose pages share g // 8, at most 1 have places with the same place // 32, and some reach 1.
All inputs are finite; a program needn't handle non-finite values.
Results may differ from a plain program's by a relative error of at most 0.035.
Values may be sent and summed in bfloat16 or wider, within the bound.
A program may use at most 128 MiB of HBM per device.

v0:
```python
import jax
import jax.numpy as jnp
from jax import lax
from jax.sharding import PartitionSpec as P

QK_NOPE = 128
QK_ROPE = 64


THETA = 50000.0
ROUTE_SCALE = 2.446
NORM_EPS = 1e-06


def joined_2(part, axis, combine):
    gathered = jax.tree.map(lambda a: lax.all_gather(a, axis), part)

    def take(source):
        return jax.tree.map(lambda a: lax.dynamic_index_in_dim(a, source, 0, False), gathered)

    return lax.fori_loop(
        1, lax.axis_size(axis), lambda source, state: combine(state, take(source)), take(0)
    )


def rotate_query(values, positions):
    half_dim = values.shape[-1] // 2
    freqs = THETA ** (-2.0 * jnp.arange(half_dim, dtype=jnp.float32) / values.shape[-1])
    angles = positions.astype(jnp.float32)[:, None] * freqs[None, :]
    cosine = jnp.cos(angles)[:, None, :]
    sine_v = jnp.sin(angles)[:, None, :]
    front = values[..., :half_dim]
    back = values[..., half_dim:]
    return jnp.concatenate(
        [front * cosine - back * sine_v, back * cosine + front * sine_v], axis=-1
    )


def pick_rows(one_page, row_ids):
    return one_page[row_ids]


def merge_parts(left_part, right_part):
    joined = jnp.maximum(left_part[0], right_part[0])
    left_factor = jnp.exp(left_part[0] - joined)
    right_factor = jnp.exp(right_part[0] - joined)
    return (
        joined,
        left_part[1] * left_factor + right_part[1] * right_factor,
        left_part[2] * left_factor[..., None] + right_part[2] * right_factor[..., None],
    )


def shards(
    hidden,
    q_weight,
    key_up,
    value_up_weight,
    out_weight,
    cache,
    page_table,
    seq_pages,
    keep_rows,
    fold_mass,
    new_place,
    norm_gain,
    router,
    routes,
    w_gate,
    w_up,
    w_down,
):
    heads_here = key_up.shape[0]
    pages_here = cache.shape[1]
    page_rows = cache.shape[2]
    latent_dim = cache.shape[3]
    kv_rank = key_up.shape[2]
    kept_count = keep_rows.shape[2]
    requests = hidden.shape[0]
    head_size = QK_NOPE + QK_ROPE
    groups = lax.axis_size("page")
    page_index = lax.axis_index("page")
    blocks = heads_here * pages_here
    sending_limit = (blocks + groups - 1) // groups
    first_page = page_index * pages_here
    partial_value = jnp.dot(hidden, q_weight, preferred_element_type=jnp.float32)
    queries = lax.psum(partial_value, "page").reshape(requests, heads_here, head_size)
    q_nope = queries[..., :QK_NOPE].astype(jnp.bfloat16)
    positions = seq_pages * page_rows - 1
    q_rope = rotate_query(queries[..., QK_NOPE:], positions).astype(jnp.bfloat16)
    q_latent = jnp.einsum(
        "rhn,hnk->rhk", q_nope, key_up, preferred_element_type=jnp.float32
    ).astype(jnp.bfloat16)
    q_full = jnp.concatenate([q_latent, q_rope], axis=-1)
    keep_here = lax.dynamic_slice_in_dim(keep_rows, first_page, pages_here, 1)
    mass_here = lax.dynamic_slice_in_dim(fold_mass, first_page, pages_here, 1)
    compact = jax.vmap(jax.vmap(pick_rows))(cache, keep_here)
    flat_rows = compact.reshape(heads_here, pages_here * kept_count, latent_dim)
    page_ends = jnp.cumsum(seq_pages)
    owner = jnp.sum((page_table[..., None] >= page_ends).astype(jnp.int32), axis=-1)
    row_owner = jnp.repeat(owner, kept_count, axis=1)
    in_request = row_owner[:, None, :] == jnp.arange(requests, dtype=jnp.int32)[None, :, None]
    scores = jnp.einsum(
        "rhk,hnk->hrn", q_full, flat_rows, preferred_element_type=jnp.float32
    ) * head_size ** (-0.5)
    row_max = jnp.max(jnp.where(in_request, scores, -1e30), axis=-1)
    row_mass = mass_here.reshape(heads_here, 1, pages_here * kept_count).astype(jnp.float32)
    weights = jnp.where(in_request, row_mass * jnp.exp(scores - row_max[..., None]), 0.0)
    totals = jnp.sum(weights, axis=-1)
    weighted = jnp.einsum(
        "hrn,hnk->hrk",
        weights.astype(jnp.bfloat16),
        flat_rows[..., :kv_rank],
        preferred_element_type=jnp.float32,
    )
    best, mass_sum, latent_sum = joined_2((row_max, totals, weighted), "page", merge_parts)
    latent_output = (latent_sum / mass_sum[..., None]).astype(jnp.bfloat16)
    head_result_rows = jnp.einsum(
        "usj,ujb->sub", latent_output, value_up_weight, preferred_element_type=jnp.float32
    ).astype(jnp.bfloat16)
    head_result_rows = head_result_rows.reshape(requests, heads_here * value_up_weight.shape[2])
    out_cols = jnp.dot(head_result_rows, out_weight, preferred_element_type=jnp.float32)
    col_width = out_cols.shape[1]
    padded = jnp.zeros((requests, col_width * groups), jnp.float32)
    padded = lax.dynamic_update_slice_in_dim(padded, out_cols, page_index * col_width, 1)
    attn_out = lax.psum(padded, ("head", "page")).astype(jnp.bfloat16)
    attn_wide = attn_out.astype(jnp.float32)
    mean_sq = jnp.mean(attn_wide * attn_wide, axis=-1, keepdims=True)
    normed = (attn_wide * lax.rsqrt(mean_sq + NORM_EPS) * norm_gain.astype(jnp.float32)).astype(
        jnp.bfloat16
    )
    logits = jnp.dot(normed, router, preferred_element_type=jnp.float32)
    picked = jax.nn.sigmoid(jnp.take_along_axis(logits, routes, axis=1))
    shares = ROUTE_SCALE * picked / jnp.sum(picked, axis=1, keepdims=True)
    expert_ids = jnp.arange(logits.shape[1], dtype=jnp.int32)
    combine = jnp.sum(
        jnp.where(routes[:, :, None] == expert_ids[None, None, :], shares[:, :, None], 0.0), axis=1
    )
    local_experts = w_gate.shape[0]
    combine_here = lax.dynamic_slice_in_dim(combine, page_index * local_experts, local_experts, 1)
    gate_part = jnp.einsum("rd,edf->erf", normed, w_gate, preferred_element_type=jnp.float32)
    up_part = jnp.einsum("rd,edf->erf", normed, w_up, preferred_element_type=jnp.float32)
    expert_hidden = (jax.nn.silu(gate_part) * up_part).astype(jnp.bfloat16)
    expert_outs = jnp.einsum(
        "erf,efd->erd", expert_hidden, w_down, preferred_element_type=jnp.float32
    )
    expert_terms = jnp.sum(combine_here.T[:, :, None] * expert_outs, axis=0)
    moe_out = lax.psum(expert_terms, ("head", "page")).astype(jnp.bfloat16)
    dest_all = new_place // blocks
    slot_all = new_place % blocks
    dest_here = lax.dynamic_slice_in_dim(dest_all, first_page, pages_here, 1).reshape(blocks)
    peer_ids = jnp.arange(groups, dtype=jnp.int32)
    dest_onehot = (dest_here[:, None] == peer_ids[None, :]).astype(jnp.int32)
    send_rank = jnp.sum(jnp.cumsum(dest_onehot, axis=0) * dest_onehot, axis=1) - 1
    send_col = dest_here * sending_limit + send_rank
    slot_ids = jnp.arange(groups * sending_limit, dtype=jnp.int32)
    chooser = (send_col[:, None] == slot_ids[None, :]).astype(jnp.bfloat16)

    def arrange(values):
        return (
            values.reshape(heads_here, groups, pages_here)
            .transpose(1, 0, 2)
            .reshape(groups, blocks)
        )

    to_here = arrange(dest_all) == page_index
    recv_rank = jnp.cumsum(to_here.astype(jnp.int32), axis=1) - 1
    recv_col = peer_ids[:, None] * sending_limit + recv_rank
    block_ids = jnp.arange(blocks, dtype=jnp.int32)
    by_slot = ((arrange(slot_all)[..., None] == block_ids) & to_here[..., None]).astype(
        jnp.bfloat16
    )
    by_col = (recv_col[..., None] == slot_ids).astype(jnp.bfloat16)
    unpack = jnp.einsum("sbq,sbc->qc", by_slot, by_col, preferred_element_type=jnp.float32).astype(
        jnp.bfloat16
    )
    owned = (slot_all.reshape(-1)[None, :] == block_ids[:, None]) & (
        dest_all.reshape(-1)[None, :] == page_index
    )
    new_mass = jnp.dot(
        owned.astype(jnp.bfloat16),
        fold_mass.reshape(-1, kept_count),
        preferred_element_type=jnp.float32,
    ).astype(jnp.bfloat16)
    payload = cache.reshape(blocks, page_rows * latent_dim)
    outgoing = jnp.einsum("bc,bx->cx", chooser, payload, preferred_element_type=jnp.float32).astype(
        jnp.bfloat16
    )
    arrived_rows = lax.all_to_all(
        outgoing.reshape(groups, sending_limit, page_rows, latent_dim),
        "page",
        split_axis=0,
        concat_axis=0,
        tiled=True,
    )
    placed = jnp.dot(
        unpack,
        arrived_rows.reshape(groups * sending_limit, page_rows * latent_dim),
        preferred_element_type=jnp.float32,
    ).astype(jnp.bfloat16)
    keep_new = jnp.dot(owned.astype(jnp.int32), keep_rows.reshape(-1, kept_count))
    new_rows = jax.vmap(pick_rows)(placed.reshape(blocks, page_rows, latent_dim), keep_new)
    return (attn_out, moe_out, new_rows, new_mass)


def solution(mesh):
    in_specs = (
        P(None, "page"),
        P("page", "head"),
        P("head", None, None),
        P("head", None, None),
        P("head", "page"),
        P("head", "page", None, None),
        P("head", "page"),
        P(),
        P("head", None, None),
        P("head", None, None),
        P("head", None),
        P(),
        P(),
        P(),
        P("page", None, "head"),
        P("page", None, "head"),
        P("page", "head", None),
    )
    out_specs = (P(), P(), P(("head", "page"), None, None), P(("head", "page"), None))
    return jax.shard_map(shards, mesh=mesh, in_specs=in_specs, out_specs=out_specs, check_vma=False)
```

profile of v0, /device:TPU:1, one launch (start us, length us, event | category | flops | bytes accessed | tf_op | source)
XLA Modules:
  0.0 995.1 jit_solution(4305672104055780673)
XLA Ops:
  7.3 1.1 constant_dynamic-slice_fusion.2
  8.6 7.8 copy.109
  16.6 249.7 %psum.21 = f32[12,4,192]{2,0,1:T(8,128)S(1)} all-reduce(f32[12,4,192]{2,0,1:T(8,128)S(1)} %copy.107), channel_id=1, replica_groups=mesh['head'=4,'page'=64] {'page'}, use_global_device_ids=true, to_apply=%region_2.3 | all-reduce | flops 9216 | bytes 73728 | tf_op jit(solution)/shard_map/psum | solution.py:87
  267.1 39.8 %gather_fusion = bf16[2048,576]{1,0:T(8,128)(2,1)} fusion(bf16[4,8,128,576]{3,2,1,0:T(8,128)(2,1)} %copy.109, s32[2048]{0:T(1024)S(1)} %reshape.256), kind=kCustom, calls=%fused_computation | custom fusion | bytes 4743168 | tf_op jit(solution)/shard_map/vmap(vmap())/gather | solution.py:40
  307.4 2.8 select_reduce_fusion
  310.2 1.1 fusion.3
  311.3 8.8 reshape.249
  320.6 8.8 convolution_convert_fusion
  329.4 15.5 %reshape.250 = bf16[64,1,128,576]{3,2,0,1:T(8,128)(2,1)} reshape(bf16[64,73728]{1,0:T(8,128)(2,1)} %convolution_convert_fusion) | data formatting | bytes 18874368 | tf_op jit(solution)/shard_map/reshape | solution.py:190
  344.8 13.9 %copy.123 = bf16[64,1,128,576]{2,3,1,0:T(8,128)(2,1)} copy(bf16[64,1,128,576]{3,2,0,1:T(8,128)(2,1)} %reshape.250) | data formatting | bytes 18874368 | tf_op jit(solution)/shard_map/reshape | solution.py:190
  358.8 10.8 %all-to-all-start = ((bf16[64,1,128,576]{2,3,1,0:T(8,128)(2,1)}), bf16[64,1,128,576]{2,3,1,0:T(8,128)(2,1)}, u32[]{:S(2)}, u32[]{:S(2)}) async-start(bf16[64,1,128,576]{2,3,1,0:T(8,128)(2,1)} %copy.123), calls=%async_computation | async-start | bytes 18874368 | tf_op jit(solution)/shard_map/all_to_all | solution.py:189
  371.6 259.3 %all-gather.4 = f32[64,4,12]{2,1,0:T(4,128)S(1)} all-gather(f32[1,4,12]{2,1,0:T(4,128)S(1)} %bitcast.156), channel_id=3, replica_groups=mesh['head'=4,'page'=64] {'page'}, dimensions={0}, use_global_device_ids=true | all-gather | bytes 12480 | tf_op jit(solution)/shard_map/all_gather | solution.py:16
  630.9 47.8 %all-gather.3 = f32[64,4,12]{2,1,0:T(4,128)S(1)} all-gather(f32[1,4,12]{2,1,0:T(4,128)S(1)} %bitcast.154), channel_id=2, replica_groups=mesh['head'=4,'page'=64] {'page'}, dimensions={0}, use_global_device_ids=true | all-gather | bytes 12480 | tf_op jit(solution)/shard_map/all_gather | solution.py:16
  680.4 66.4 %while.19 = (s32[]{:T(128)}, f32[4,12]{1,0:T(4,128)S(1)}, f32[4,12]{1,0:T(4,128)S(1)}, f32[4,12,512]{2,1,0:T(8,128)S(1)}, f32[64,4,12]{2,1,0:T(4,128)S(1)}, /*in...) while((s32[]{:T(128)}, f32[4,12]{1,0:T(4,128)S(1)}, ...), condition=%wide.region_6.7_spmd, body=%wide.region_5.6_spmd.sunk | while | flops 74021 | bytes 296983 | solution.py:21
  680.5 1.0 fusion.118
  681.5 1.0 fusion.118
  682.6 1.0 fusion.118
  683.6 1.0 fusion.118
  684.7 1.0 fusion.118
  685.7 1.0 fusion.118
  686.8 1.0 fusion.118
  687.9 1.0 fusion.118
  690.0 1.0 fusion.118
  692.1 1.0 fusion.118
  694.2 1.0 fusion.118
  696.3 1.0 fusion.118
  698.4 1.0 fusion.118
  699.5 1.0 fusion.118
  700.5 1.0 fusion.118
  701.6 1.0 fusion.118
  702.6 1.0 fusion.118
  703.7 1.0 fusion.118
  704.7 1.0 fusion.118
  705.8 1.0 fusion.118
  706.8 1.0 fusion.118
  707.9 1.0 fusion.118
  710.0 1.0 fusion.118
  712.1 1.0 fusion.118
  714.2 1.0 fusion.118
  716.3 1.0 fusion.118
  718.4 1.0 fusion.118
  719.5 1.0 fusion.118
  720.5 1.0 fusion.118
  721.6 1.0 fusion.118
  722.6 1.0 fusion.118
  723.7 1.0 fusion.118
  724.8 1.0 fusion.118
  725.8 1.0 fusion.118
  726.9 1.0 fusion.118
  727.9 1.0 fusion.118
  730.0 1.0 fusion.118
  732.1 1.0 fusion.118
  734.2 1.0 fusion.118
  736.4 1.0 fusion.118
  746.9 1.3 fusion.23
  748.7 75.9 %psum.22 = bf16[12,2048]{1,0:T(8,128)(2,1)S(1)} all-reduce(f32[12,2048]{1,0:T(8,128)S(1)} %dynamic_update_slice.3), channel_id=1, replica_groups=mesh['head'=4,'page'=64] {'head','page'}, use_global_device_ids=true, to_apply=%region_7.8 | all-reduce | flops 24576 | bytes 147456 | tf_op jit(solution)/shard_map/psum | solution.py:126
  825.0 1.7 gather_fusion.1
  827.8 2.5 convolution_multiply_fusion
  830.3 74.2 %psum.23 = bf16[12,2048]{1,0:T(8,128)(2,1)} all-reduce(f32[12,2048]{1,0:T(8,128)S(1)} %convolution_multiply_fusion), channel_id=1, replica_groups=mesh['head'=4,'page'=64] {'head','page'}, use_global_device_ids=true, to_apply=%region_11.12 | all-reduce | flops 24576 | bytes 147456 | tf_op jit(solution)/shard_map/psum | solution.py:148
  904.5 14.1 %copy.124 = bf16[64,1,128,576]{3,2,0,1:T(8,128)(2,1)} copy(bf16[64,1,128,576]{2,3,1,0:T(8,128)(2,1)} %all-to-all-done) | data formatting | bytes 18874368 | tf_op jit(solution)/shard_map/all_to_all | solution.py:189
  918.6 15.3 %reshape.251 = bf16[64,73728]{1,0:T(8,128)(2,1)} reshape(bf16[64,1,128,576]{3,2,0,1:T(8,128)(2,1)} %copy.124) | data formatting | bytes 18874368 | tf_op jit(solution)/shard_map/reshape | solution.py:198
  933.8 8.0 convolution_convert_fusion.1
  941.9 8.8 reshape.252
  950.7 37.5 %gather_fusion.2 = bf16[2048,576]{1,0:T(8,128)(2,1)} fusion(bf16[32,128,576]{2,1,0:T(8,128)(2,1)} %reshape.252, s32[2048]{0:T(1024)S(1)} %reshape.268), kind=kCustom, calls=%fused_computation.2 | custom fusion | bytes 4734976 | tf_op jit(solution)/shard_map/vmap()/gather | solution.py:40
  (192 shorter events, 32.6 us)
Async XLA Ops:
  7.2 820.7 %copy-start = (bf16[1,352,2048]{2,1,0:T(8,128)(2,1)S(1)}, bf16[1,352,2048]{2,1,0:T(8,128)(2,1)}, u32[]{:S(2)}) copy-start(bf16[1,352,2048]{2,1,0:T(8,128)(2,1)} %param.35) | copy-start | bytes 4325380
  7.2 672.3 %all-gather.7.cloned.1.call-start = ((), (), s32[]{:S(2)}) async-start(), calls=%async_computation.1 | async-start | bytes 8519680 | tf_op jit(solution)/shard_map/all_gather | solution.py:16
  8.5 7.8 copy-start.8
  8.5 7.8 copy-start.11
  8.5 257.7 %copy-start.15 = (s32[12]{0:T(128)S(1)}, s32[12]{0:T(128)}, u32[]{:S(2)}) copy-start(s32[12]{0:T(128)} %param.26) | copy-start | bytes 148
  8.5 257.9 %copy-start.13 = (s32[4,8]{1,0:T(4,128)S(1)}, s32[4,8]{1,0:T(4,128)}, u32[]{:S(2)}) copy-start(s32[4,8]{1,0:T(4,128)} %param.25) | copy-start | bytes 388
  8.5 258.3 %copy-start.6 = (bf16[4,512,64]{1,2,0:T(8,128)(2,1)S(1)}, bf16[4,512,64]{1,2,0:T(8,128)(2,1)}, u32[]{:S(2)}) copy-start(bf16[4,512,64]{1,2,0:T(8,128)(2,1)} %param.28) | copy-start | bytes 786436
  267.1 40.0 %copy-start.5 = (bf16[4,128,512]{2,1,0:T(8,128)(2,1)S(1)}, bf16[4,128,512]{2,1,0:T(8,128)(2,1)}, u32[]{:S(2)}) copy-start(bf16[4,128,512]{2,1,0:T(8,128)(2,1)} %param.21) | copy-start | bytes 1572868
  307.0 3.2 copy-start.1
  311.3 8.8 copy-start.7
  358.8 10.8 %copy-start.12 = (bf16[2048]{0:T(1024)(128)(2,1)S(1)}, bf16[2048]{0:T(1024)(128)(2,1)}, u32[]{:S(2)}) copy-start(bf16[2048]{0:T(1024)(128)(2,1)} %param.30) | copy-start | bytes 12292
  358.8 10.8 %copy-start.9 = (s32[12,6]{0,1:T(8,128)S(1)}, s32[12,6]{0,1:T(8,128)}, u32[]{:S(2)}) copy-start(s32[12,6]{0,1:T(8,128)} %param.32) | copy-start | bytes 868
  358.8 12.1 %copy-start.4 = (s32[4,512,64]{1,2,0:T(8,128)S(1)}, s32[4,512,64]{1,2,0:T(8,128)}, u32[]{:S(2)}) copy-start(s32[4,512,64]{1,2,0:T(8,128)} %param.27) | copy-start | bytes 1572868
  358.8 545.7 %all-to-all-start = ((bf16[64,1,128,576]{2,3,1,0:T(8,128)(2,1)}), bf16[64,1,128,576]{2,3,1,0:T(8,128)(2,1)}, u32[]{:S(2)}, u32[]{:S(2)}) async-start(bf16[64,1,128,576]{2,3,1,0:T(8,128)(2,1)} %copy.123), calls=%async_computation | async-start | bytes 18874368 | tf_op jit(solution)/shard_map/all_to_all | solution.py:189
  370.9 377.3 %copy-start.10 = (bf16[512,32]{0,1:T(8,128)(2,1)S(1)}, bf16[512,32]{0,1:T(8,128)(2,1)}, u32[]{:S(2)}) copy-start(bf16[512,32]{0,1:T(8,128)(2,1)} %param.23) | copy-start | bytes 98308
  371.4 453.3 %copy-start.14 = (bf16[2048,64]{0,1:T(8,128)(2,1)S(1)}, bf16[2048,64]{0,1:T(8,128)(2,1)}, u32[]{:S(2)}) copy-start(bf16[2048,64]{0,1:T(8,128)(2,1)} %param.31) | copy-start | bytes 786436
  824.6 3.2 copy-start.3
  825.0 2.3 copy-start.2
Sparse Core Ops, SparseCore 0:
  311.4 121.0 all-gather.6
where the time goes:
time: 999 us; the launch traced here: 995 us
  blocking collectives  707 us (71%)
  local copies, waits for them, and re-layouts  168 us (17%)
  other arithmetic  66.3 us (7%)
  matrix products  26.8 us (3%)
  between operations  14.4 us (1%)
  starting transfers between devices  10.8 us (1%)
    all_gather x2, blocking collectives, joined_2(): gathered = jax.tree.map(lambda a: lax.all_gather(a, axis), part)  307 us
    psum x1, blocking collectives, shards(): lax.psum(partial_value, 'page').reshape(requests, heads_here, head_size)  250 us
    gather x4, local copies, waits for them, and re-layouts, pick_rows(): return one_page[row_ids]  77.5 us
    psum x1, blocking collectives, shards(): attn_out = lax.psum(padded, ('head', 'page')).astype(jnp.bfloat16)  75.9 us
    psum x1, blocking collectives, shards(): moe_out = lax.psum(expert_terms, ('head', 'page')).astype(jnp.bfloat16)  74.2 us
    add x63, other arithmetic, merge_parts(): left_part[2] * left_factor[..., None]  62.9 us
    reshape x2, local copies, waits for them, and re-layouts, shards(): outgoing.reshape(groups, sending_limit, page_rows, latent_dim)  29.4 us
  transfers between devices with their start and end apart: 2, of which 0 were waited for; matrix products, arithmetic and copies ran while one was open for 12% of the time, Pallas kernels for 0%

commit v1 on v0

v1 whole, which is shorter than its diff:
```python
import functools

import jax
import jax.numpy as jnp
from jax import lax
from jax.experimental import pallas as pl
from jax.experimental.pallas import tpu as pltpu
from jax.sharding import PartitionSpec as P

QK_NOPE = 128
QK_ROPE = 64
THETA = 50000.0
ROUTE_SCALE = 2.446
NORM_EPS = 1e-06
NEG = -1e30

MESH = pl.DeviceIdType.MESH
F32 = jnp.float32
BF16 = jnp.bfloat16

HERE = 4
PAGES = 8
BLOCKS = HERE * PAGES
ROWS = 128
KEPT = 64
RANK = 512
LATENT = 576
REQ = 12
GROUPS = 64
NX = 4
PACK = (144, 256)


def dot(a, b, dims=(((1,), (0,)), ((), ()))):
    return lax.dot_general(a, b, dims, preferred_element_type=F32)


def compact_kernel(dest_ref, keep_ref, cache_ref, flat_ref, send_ref, pages, packed, in_sem, out_sem):
    def fetch(b):
        return pltpu.make_async_copy(
            cache_ref.at[b // PAGES, b % PAGES], pages.at[b], in_sem.at[b]
        )

    def put(b):
        return pltpu.make_async_copy(packed.at[b], send_ref.at[dest_ref[b]], out_sem.at[b])

    def start(b, carry):
        fetch(b).start()
        return carry

    lax.fori_loop(0, BLOCKS, start, 0)

    def step(b, carry):
        fetch(b).wait()
        row = lax.broadcasted_iota(jnp.int32, (ROWS, KEPT), 0)
        chosen = (row == keep_ref[pl.ds(b, 1), :]).astype(F32).astype(BF16)
        rows = dot(chosen, pages[b], (((0,), (0,)), ((), ())))
        flat_ref[b] = rows.astype(BF16)
        packed[b, 0:64] = rows[:, 0:256].astype(BF16)
        packed[b, 64:128] = rows[:, 256:512].astype(BF16)
        rope = rows[:, 512:576]
        packed[b, 128:144] = jnp.concatenate(
            [rope[16 * g : 16 * g + 16] for g in range(4)], axis=1
        ).astype(BF16)
        put(b).start()
        return carry

    lax.fori_loop(0, BLOCKS, step, 0)

    def finish(b, carry):
        put(b).wait()
        return carry

    lax.fori_loop(0, BLOCKS, finish, 0)


def compact_blocks(dest, keep, cache):
    return pl.pallas_call(
        compact_kernel,
        out_shape=(
            jax.ShapeDtypeStruct((BLOCKS, KEPT, LATENT), BF16),
            jax.ShapeDtypeStruct((GROUPS, *PACK), BF16),
        ),
        in_specs=[
            pl.BlockSpec(memory_space=pltpu.SMEM),
            pl.BlockSpec(memory_space=pltpu.VMEM),
            pl.BlockSpec(memory_space=pl.ANY),
        ],
        out_specs=(pl.BlockSpec(memory_space=pltpu.VMEM), pl.BlockSpec(memory_space=pl.ANY)),
        scratch_shapes=[
            pltpu.VMEM((BLOCKS, ROWS, LATENT), BF16),
            pltpu.VMEM((BLOCKS, *PACK), BF16),
            pltpu.SemaphoreType.DMA((BLOCKS,)),
            pltpu.SemaphoreType.DMA((BLOCKS,)),
        ],
        compiler_params=pltpu.CompilerParams(vmem_limit_bytes=24 << 20),
        name="compact_blocks",
    )(dest, keep, cache)


def place_kernel(src_ref, recv_ref, rows_ref, held, in_sem):
    def fetch(q):
        return pltpu.make_async_copy(recv_ref.at[src_ref[q]], held.at[q], in_sem.at[q])

    def start(q, carry):
        fetch(q).start()
        return carry

    lax.fori_loop(0, BLOCKS, start, 0)

    def step(q, carry):
        fetch(q).wait()
        rows_ref[q, :, 0:256] = held[q, 0:64]
        rows_ref[q, :, 256:512] = held[q, 64:128]
        rope = held[q, 128:144].astype(F32)
        rows_ref[q, :, 512:576] = jnp.concatenate(
            [rope[:, 64 * g : 64 * g + 64] for g in range(4)], axis=0
        ).astype(BF16)
        return carry

    lax.fori_loop(0, BLOCKS, step, 0)


def place_blocks(src, recv):
    return pl.pallas_call(
        place_kernel,
        out_shape=jax.ShapeDtypeStruct((BLOCKS, KEPT, LATENT), BF16),
        in_specs=[pl.BlockSpec(memory_space=pltpu.SMEM), pl.BlockSpec(memory_space=pl.ANY)],
        out_specs=pl.BlockSpec(memory_space=pltpu.VMEM),
        scratch_shapes=[pltpu.VMEM((BLOCKS, *PACK), BF16), pltpu.SemaphoreType.DMA((BLOCKS,))],
        compiler_params=pltpu.CompilerParams(vmem_limit_bytes=16 << 20),
        name="place_blocks",
    )(src, recv)


OFFSETS = [
    (dy, sign * dz, dc)
    for dz in range(5)
    for dy in range(4)
    for dc in range(2)
    for sign in ((1,) if dz in (0, 4) else (1, -1))
    if (dy, dz, dc) != (0, 0, 0)
]
FEED = (2,) * 13


def split3(v):
    a = v.astype(BF16)
    rest = v - a.astype(F32)
    b = rest.astype(BF16)
    return a, b, (rest - b.astype(F32)).astype(BF16)


def decode_kernel(
    hidden_ref,
    qw_ref,
    owner_ref,
    mass_ref,
    cos_ref,
    sin_ref,
    gain_ref,
    routes_ref,
    key_hbm,
    value_hbm,
    out_hbm,
    flat_hbm,
    router_hbm,
    gate_hbm,
    up_hbm,
    down_hbm,
    send_ref,
    attn_ref,
    moe_ref,
    recv_ref,
    key_v,
    value_v,
    outw_v,
    flat_v,
    router_v,
    gate_v,
    up_v,
    down_v,
    q_out,
    q_in,
    q2_out,
    q2_in,
    q3_out,
    q3_in,
    a_out,
    a_in,
    b_out,
    b_in,
    c_out,
    c_in,
    d_out,
    d_in,
    d2_out,
    d2_in,
    d3_out,
    d3_in,
    e_out,
    e_in,
    e2_out,
    e2_in,
    e3_out,
    e3_in,
    e4_out,
    e4_in,
    load_sem,
    own_sem,
    small_send,
    small_recv,
    bulk_send,
    bulk_recv,
):
    x = lax.axis_index("head")
    p = lax.axis_index("page")
    y, z, c = p // 16, (p // 2) % 8, p % 2
    a = y * 2 + c

    loads = [
        pltpu.make_async_copy(src, dst, load_sem.at[n])
        for n, (src, dst) in enumerate(
            (
                (key_hbm, key_v),
                (flat_hbm, flat_v),
                (value_hbm, value_v),
                (out_hbm, outw_v),
                (router_hbm, router_v),
                (gate_hbm.at[0], gate_v),
                (up_hbm.at[0], up_v),
                (down_hbm.at[0], down_v),
            )
        )
    ]
    for load in loads:
        load.start()
    own = pltpu.make_async_copy(send_ref.at[p], recv_ref.at[p], own_sem)
    own.start()

    barrier = pltpu.get_barrier_semaphore()

    def greet(k, carry):
        pl.semaphore_signal(
            barrier, inc=1, device_id=(x, (p + k) % GROUPS), device_id_type=MESH
        )
        return carry

    lax.fori_loop(1, GROUPS, greet, 0)
    for k in range(1, NX):
        pl.semaphore_signal(barrier, inc=1, device_id=((x + k) % NX, p), device_id_type=MESH)

    part = dot(hidden_ref[...], qw_ref[...])
    width = QK_NOPE + QK_ROPE
    for h in range(HERE):
        q_out[h] = part[:, width * h : width * h + QK_NOPE]
    for n in range(2):
        q_out[HERE + n] = jnp.concatenate(
            [
                part[:, width * h + QK_NOPE : width * (h + 1)]
                for h in (2 * n, 2 * n + 1)
            ],
            axis=1,
        )
    q_out[6] = jnp.zeros_like(q_out[6])
    q_out[7] = jnp.zeros_like(q_out[7])

    pl.semaphore_wait(barrier, GROUPS - 1 + NX - 1)

    fed = []

    def bulk(offset):
        dy, dz, dc = offset
        n = OFFSETS.index(offset)
        to = ((y + dy) % 4) * 16 + ((z + dz + 8) % 8) * 2 + (c + dc) % 2
        return pltpu.make_async_remote_copy(
            send_ref.at[to],
            recv_ref.at[p],
            bulk_send.at[n],
            bulk_recv.at[n],
            device_id=(x, to),
            device_id_type=MESH,
        )

    def feed(count):
        for offset in OFFSETS[len(fed) : len(fed) + count]:
            bulk(offset).start()
            fed.append(offset)

    smalls = []

    def exchange(stage, kind, out, into, scatter):
        copies = []
        size = NX if kind == "x" else 8
        me = {"a": a, "z": z, "x": x}[kind]
        for k in range(1, size):
            other = (me + k) % size
            if kind == "a":
                target = (x, (other // 2) * 16 + z * 2 + other % 2)
            elif kind == "z":
                target = (x, y * 16 + other * 2 + c)
            else:
                target = (other, p)
            copies.append(
                pltpu.make_async_remote_copy(
                    out.at[other] if scatter else out,
                    into.at[me],
                    small_send.at[stage, k],
                    small_recv.at[stage, k],
                    device_id=target,
                    device_id_type=MESH,
                )
            )
        for copy in copies:
            copy.start()
        into[me] = out[me] if scatter else out[...]
        feed(FEED[stage])
        for copy in copies:
            copy.wait_recv()
        smalls.extend(copies)

    def added(into, size):
        total = into[0].astype(F32)
        for n in range(1, size):
            total = total + into[n].astype(F32)
        return total

    exchange(0, "a", q_out, q_in, True)
    q2_out[...] = added(q_in, 8)
    exchange(1, "z", q2_out, q2_in, False)
    mine = added(q2_in, 8)
    lane = lax.broadcasted_iota(jnp.int32, mine.shape, 1)
    turned = jnp.where(lane % 64 < 32, pltpu.roll(mine, 96, 1), pltpu.roll(mine, 32, 1))
    rotated = mine * cos_ref[...] + turned * sin_ref[...]
    q3_out[...] = jnp.where(a < HERE, mine, rotated).astype(BF16)
    exchange(2, "a", q3_out, q3_in, False)

    loads[0].wait()
    loads[1].wait()
    scale = width ** (-0.5)
    rows_here = PAGES * KEPT
    request = lax.broadcasted_iota(jnp.int32, (REQ, rows_here), 0)
    for h in range(HERE):
        rope = q3_in[HERE + h // 2][:, 64 * (h % 2) : 64 * (h % 2) + 64]
        latent_query = dot(q3_in[h], key_v[h]).astype(BF16)
        block = flat_v[h]
        nt = (((1,), (1,)), ((), ()))
        scores = (dot(latent_query, block[:, :RANK], nt) + dot(rope, block[:, RANK:], nt)) * scale
        mine_here = owner_ref[h : h + 1, :] == request
        best = jnp.max(jnp.where(mine_here, scores, NEG), axis=1, keepdims=True)
        weights = jnp.where(mine_here, mass_ref[h : h + 1, :] * jnp.exp(scores - best), 0.0)
        total = jnp.sum(weights, axis=1, keepdims=True)
        summed = dot(weights.astype(BF16), block[:, :RANK])
        stats = jnp.concatenate(
            [
                jnp.broadcast_to(v.astype(F32), (REQ, 16))
                for v in (*split3(best), *split3(total))
            ]
            + [jnp.zeros((REQ, 32), F32)],
            axis=1,
        ).astype(BF16)
        for half in range(2):
            a_out[2 * h + half, :, 0:256] = summed[:, 256 * half : 256 * half + 256].astype(BF16)
            a_out[2 * h + half, :, 256:384] = stats

    def merged(into):
        def stat(n, first):
            return sum(
                into[n, :, 256 + 16 * s : 256 + 16 * s + 16].astype(F32)[:, 0:1]
                for s in range(first, first + 3)
            )

        bests = [stat(n, 0) for n in range(8)]
        best = functools.reduce(jnp.maximum, bests)
        total = jnp.zeros((REQ, 1), F32)
        latent = jnp.zeros((REQ, 256), F32)
        for n in range(8):
            factor = jnp.exp(bests[n] - best)
            total = total + factor * stat(n, 3)
            latent = latent + factor * into[n, :, 0:256].astype(F32)
        return best, total, latent

    exchange(3, "a", a_out, a_in, True)
    best, total, latent = merged(a_in)
    b_out[:, 0:256] = latent.astype(BF16)
    b_out[:, 256:384] = jnp.concatenate(
        [jnp.broadcast_to(v.astype(F32), (REQ, 16)) for v in (*split3(best), *split3(total))]
        + [jnp.zeros((REQ, 32), F32)],
        axis=1,
    ).astype(BF16)
    exchange(4, "z", b_out, b_in, False)
    _, total, latent = merged(b_in)
    latent_out = (latent / total).astype(BF16)
    loads[2].wait()
    c_out[...] = dot(latent_out, value_v[a // 2, pl.ds((a % 2) * 256, 256), :])
    exchange(5, "a", c_out, c_in, False)

    loads[3].wait()
    cols = jnp.zeros((REQ, 32), F32)
    for h in range(HERE):
        head_out = (c_in[2 * h] + c_in[2 * h + 1]).astype(BF16)
        cols = cols + dot(head_out, outw_v[128 * h : 128 * h + 128, :])
    spread = jnp.concatenate([cols] * 4, axis=1)
    lane = lax.broadcasted_iota(jnp.int32, spread.shape, 1)
    d_out[...] = jnp.where(lane // 32 == p % 4, spread, 0.0)
    exchange(6, "x", d_out, d_in, False)
    d2_out[...] = added(d_in, NX).astype(BF16)
    exchange(7, "z", d2_out, d2_in, False)
    for n in range(4):
        d3_out[n] = (d2_in[2 * n].astype(F32) + d2_in[2 * n + 1].astype(F32)).astype(BF16)
    exchange(8, "a", d3_out, d3_in, False)

    tiles = [
        d3_in[2 * (t // 4), t % 4].astype(F32) + d3_in[2 * (t // 4) + 1, t % 4].astype(F32)
        for t in range(16)
    ]
    square = jnp.zeros((REQ, 128), F32)
    for t in range(16):
        attn_ref[:, 128 * t : 128 * t + 128] = tiles[t].astype(BF16)
        square = square + tiles[t] * tiles[t]
    mean = jnp.sum(square, axis=1, keepdims=True) * (1.0 / 2048)
    inverse = lax.rsqrt(mean + NORM_EPS)
    normed = jnp.concatenate(
        [
            (tiles[t] * inverse * gain_ref[:, 128 * t : 128 * t + 128].astype(F32)).astype(BF16)
            for t in range(16)
        ],
        axis=1,
    )

    loads[4].wait()
    logits = dot(normed, router_v[...])
    chance = 1.0 / (1.0 + jnp.exp(-logits))
    expert = lax.broadcasted_iota(jnp.int32, chance.shape, 1)
    routed = jnp.zeros(chance.shape, F32)
    for t in range(routes_ref.shape[1]):
        routed = jnp.where(routes_ref[:, t : t + 1] == expert, 1.0, routed)
    chosen = routed * chance
    share = ROUTE_SCALE * chosen / jnp.sum(chosen, axis=1, keepdims=True)
    share_here = jnp.sum(jnp.where(expert == p, share, 0.0), axis=1, keepdims=True)
    loads[5].wait()
    gate = dot(normed, gate_v[...])
    loads[6].wait()
    up = dot(normed, up_v[...])
    expert_hidden = (gate / (1.0 + jnp.exp(-gate)) * up).astype(BF16)
    loads[7].wait()
    for n in range(8):
        e_out[n] = (
            share_here * dot(expert_hidden, down_v[:, 256 * n : 256 * n + 256])
        ).astype(BF16)
    exchange(9, "a", e_out, e_in, True)
    e2_out[...] = added(e_in, 8).astype(BF16)
    exchange(10, "z", e2_out, e2_in, False)
    e3_out[...] = added(e2_in, 8).astype(BF16)
    exchange(11, "x", e3_out, e3_in, False)
    e4_out[...] = added(e3_in, NX).astype(BF16)
    exchange(12, "a", e4_out, e4_in, False)
    for n in range(8):
        moe_ref[:, 256 * n : 256 * n + 256] = e4_in[n]

    feed(len(OFFSETS))
    for copy in smalls:
        copy.wait_send()
    own.wait()
    for offset in OFFSETS:
        bulk(offset).wait()


def decode(*operands):
    big = [pl.BlockSpec(memory_space=pl.ANY)] * 9
    small = [pl.BlockSpec(memory_space=pltpu.VMEM)] * 8
    tile = (REQ, 128)
    wide = (REQ, 256)
    stat = (REQ, 384)

    def pair(shape, parts, dtype, scatter):
        return [
            pltpu.VMEM((parts, *shape) if scatter else shape, dtype),
            pltpu.VMEM((parts, *shape), dtype),
        ]

    return pl.pallas_call(
        decode_kernel,
        out_shape=(
            jax.ShapeDtypeStruct((REQ, 2048), BF16),
            jax.ShapeDtypeStruct((REQ, 2048), BF16),
            jax.ShapeDtypeStruct((GROUPS, *PACK), BF16),
        ),
        in_specs=small + big,
        out_specs=(
            pl.BlockSpec(memory_space=pltpu.VMEM),
            pl.BlockSpec(memory_space=pltpu.VMEM),
            pl.BlockSpec(memory_space=pl.ANY),
        ),
        scratch_shapes=[
            pltpu.VMEM((HERE, QK_NOPE, RANK), BF16),
            pltpu.VMEM((HERE, RANK, 128), BF16),
            pltpu.VMEM((512, 32), BF16),
            pltpu.VMEM((HERE, PAGES * KEPT, LATENT), BF16),
            pltpu.VMEM((2048, 64), BF16),
            pltpu.VMEM((2048, 352), BF16),
            pltpu.VMEM((2048, 352), BF16),
            pltpu.VMEM((352, 2048), BF16),
            *pair(tile, 8, F32, True),
            *pair(tile, 8, F32, False),
            *pair(tile, 8, BF16, False),
            *pair(stat, 8, BF16, True),
            *pair(stat, 8, BF16, False),
            *pair(tile, 8, F32, False),
            *pair(tile, NX, F32, False),
            *pair(tile, 8, BF16, False),
            *pair((4, *tile), 8, BF16, False),
            *pair(wide, 8, BF16, True),
            *pair(wide, 8, BF16, False),
            *pair(wide, NX, BF16, False),
            *pair(wide, 8, BF16, False),
            pltpu.SemaphoreType.DMA((8,)),
            pltpu.SemaphoreType.DMA,
            pltpu.SemaphoreType.DMA((13, 8)),
            pltpu.SemaphoreType.DMA((13, 8)),
            pltpu.SemaphoreType.DMA((GROUPS,)),
            pltpu.SemaphoreType.DMA((GROUPS,)),
        ],
        compiler_params=pltpu.CompilerParams(
            collective_id=0, has_side_effects=True, vmem_limit_bytes=40 << 20
        ),
        name="decode",
    )(*operands)


def shards(
    hidden,
    q_weight,
    key_up,
    value_up_weight,
    out_weight,
    cache,
    page_table,
    seq_pages,
    keep_rows,
    fold_mass,
    new_place,
    norm_gain,
    router,
    routes,
    w_gate,
    w_up,
    w_down,
):
    page_index = lax.axis_index("page")
    first_page = page_index * PAGES

    def here(array):
        return lax.dynamic_slice_in_dim(array, first_page, PAGES, 1)

    dest = here(new_place).reshape(BLOCKS) // BLOCKS
    keep = here(keep_rows).reshape(BLOCKS, KEPT)
    flat, send = compact_blocks(dest, keep, cache)

    page_ends = jnp.cumsum(seq_pages)
    owner = jnp.sum((page_table[..., None] >= page_ends).astype(jnp.int32), axis=-1)
    row_owner = jnp.repeat(owner, KEPT, axis=1)
    row_mass = here(fold_mass).reshape(HERE, PAGES * KEPT).astype(F32)
    positions = seq_pages * ROWS - 1
    half = QK_ROPE // 2
    freqs = THETA ** (-2.0 * jnp.arange(half, dtype=F32) / QK_ROPE)
    angles = positions.astype(F32)[:, None] * freqs[None, :]
    cosine = jnp.tile(jnp.cos(angles), (1, 4))
    sine = jnp.sin(angles)
    sine = jnp.concatenate([-sine, sine, -sine, sine], axis=1)

    attn_out, moe_out, recv = decode(
        hidden,
        q_weight,
        row_owner,
        row_mass,
        cosine,
        sine,
        norm_gain.reshape(1, -1),
        routes,
        key_up,
        value_up_weight,
        out_weight,
        flat.reshape(HERE, PAGES * KEPT, LATENT),
        router,
        w_gate,
        w_up,
        w_down,
        send,
    )

    slots = page_index * BLOCKS + jnp.arange(BLOCKS, dtype=jnp.int32)
    owned = slots[:, None] == new_place.reshape(1, -1)
    source = jnp.arange(GROUPS * PAGES, dtype=jnp.int32) // PAGES
    src = jnp.sum(jnp.where(owned, jnp.tile(source, HERE)[None, :], 0), axis=1)
    new_mass = jnp.dot(
        owned.astype(BF16), fold_mass.reshape(-1, KEPT), preferred_element_type=F32
    ).astype(BF16)
    new_rows = place_blocks(src, recv)
    return (attn_out, moe_out, new_rows, new_mass)


def solution(mesh):
    in_specs = (
        P(None, "page"),
        P("page", "head"),
        P("head", None, None),
        P("head", None, None),
        P("head", "page"),
        P("head", "page", None, None),
        P("head", "page"),
        P(),
        P("head", None, None),
        P("head", None, None),
        P("head", None),
        P(),
        P(),
        P(),
        P("page", None, "head"),
        P("page", None, "head"),
        P("page", "head", None),
    )
    out_specs = (P(), P(), P(("head", "page"), None, None), P(("head", "page"), None))
    return jax.shard_map(shards, mesh=mesh, in_specs=in_specs, out_specs=out_specs, check_vma=False)
```

time: 999 us -> 232 us (0.23)
  the two profiles are of different devices: /device:TPU:1 before, /device:TPU:123 now
where the time goes in v1:
time: 232 us; the launch traced here: 231 us
  Pallas kernels  194 us (84%)
  local copies, waits for them, and re-layouts  34.4 us (15%)
    pallas_call x1, Pallas kernels, decode(): pl.pallas_call(decode_kernel, out_shape=(jax.ShapeDtypeStruct((REQ, 2048)...  167 us
    unnamed x52, local copies, waits for them, and re-layouts  32.1 us
    pallas_call x1, Pallas kernels, compact_blocks(): pl.pallas_call(compact_kernel, out_shape=(jax.ShapeDtypeStruct((BLOCKS, K...  19.6 us
    pallas_call x1, Pallas kernels, place_blocks(): pl.pallas_call(place_kernel, out_shape=jax.ShapeDtypeStruct((BLOCKS, KEPT...  8.09 us

profile of v1, /device:TPU:123, one launch (start us, length us, event | category | flops | bytes accessed | tf_op | source)
XLA Modules:
  0.0 231.4 jit_solution(7658058158247190235)
XLA Ops:
  0.6 0.0 copy-start
  0.7 1.0 copy-done
  1.7 0.1 constant_dynamic-slice_fusion
  1.8 0.1 copy.48
  1.9 0.8 constant_dynamic-slice_fusion.1
  2.6 0.1 reshape.113
  2.7 7.7 %copy.49.cache_ref = bf16[4,8,128,576]{3,2,1,0:T(8,128)(2,1)} copy(bf16[4,8,128,576]{2,3,1,0:T(8,128)(2,1)} %param.22) | data formatting | bytes 9437184 | tf_op args[5]
  10.4 0.0 copy-start.1
  10.4 2.5 %copy-done.1 = bf16[4,8,128,576]{3,2,1,0:T(8,128)(2,1)S(1)} copy-done((bf16[4,8,128,576]{3,2,1,0:T(8,128)(2,1)S(1)}, bf16[4,8,128,576]{3,2,1,0:T(8,128)(2,1)}, u32[]{:S(2)}) %copy-start.1) | copy-done | bytes 4718616
  12.9 0.0 copy-start.19
  12.9 19.6 %compact_blocks.1 = (bf16[32,64,576]{2,1,0:T(8,128)(2,1)S(1)}, bf16[64,144,256]{2,1,0:T(8,128)(2,1)S(1)}) custom-call(s32[32]{0:T(128)S(1)} %and_select_fusion.dest_ref, s32[32,64]{1,0:T(8,128)S(1)} %bitcast.13, bf16[4,8,128,576]{3,2,1,0:T(8,128)(2,1)S(1)} %copy-done.1), custom_call_target="tpu_custom_call" | custom-call | tf_op jit(solution)/shard_map/compact_blocks/pallas_call | solution.py:78
  32.5 0.0 copy-start.3
  32.5 2.1 copy-done.3
  34.6 0.0 copy-start.6
  34.6 1.5 copy-done.6
  36.1 0.9 constant_dynamic-slice_fusion.2
  37.1 0.1 copy.56
  37.1 0.1 reshape.117.mass_ref
  37.2 0.0 copy-done.19
  37.3 0.1 fusion.4
  37.4 0.1 pad_maximum_fusion.sin_ref
  37.5 0.1 tile.7.cos_ref
  37.6 1.8 copy.53.gate_hbm
  39.4 0.0 copy-start.14
  39.4 0.0 copy-start.18
  39.4 0.0 copy-start.16
  39.4 0.0 copy-start.17
  39.5 0.0 copy-start.9
  39.5 0.0 copy-start.11
  39.5 0.0 copy-start.12
  39.5 2.6 %copy.54.up_hbm = bf16[1,2048,352]{2,1,0:T(8,128)(2,1)} copy(bf16[1,2048,352]{1,2,0:T(8,128)(2,1)} %param.32) | data formatting | bytes 2883584 | tf_op args[15]
  42.1 1.2 copy.52.router_hbm
  43.4 0.0 copy-done.14
  43.4 0.1 copy.51.out_hbm
  43.5 0.2 reduce-window.8
  43.7 0.0 copy-done.18
  43.7 0.2 convert_reduce_fusion
  43.9 0.1 broadcast_in_dim.22
  44.0 0.1 reshape.111.owner_ref
  44.0 0.0 copy-done.16
  44.0 0.1 copy.50.routes_ref
  44.1 0.0 copy-done.17
  44.2 0.0 copy-done.9
  44.2 0.0 copy-done.11
  44.2 0.0 copy-done.12
  44.2 0.0 copy-start.2
  44.2 1.4 copy-done.2
  45.6 0.0 copy-start.7
  45.6 1.7 copy-done.7
  47.3 0.0 copy-start.8
  47.3 1.4 copy-done.8
  48.7 0.0 copy-start.10
  48.7 1.0 copy-done.10
  49.8 166.6 %decode.1 = (bf16[12,2048]{1,0:T(8,128)(2,1)S(1)}, bf16[12,2048]{1,0:T(8,128)(2,1)S(1)}, bf16[64,144,256]{2,1,0:T(8,128)(2,1)S(1)}) custom-call(bf16[12,32]{1,0:T(8,128)(2,1)S(1)} %copy-done.12, bf16[32,768]{1,0:T(8,128)(2,1)S(1)} %copy-done.11, s32[4,512]{1,0:T(4,128)S(1)} %reshape.111.owner_ref, f32[4,512]{1,0:T(4,128)S(1)} %reshape.117.mass_ref, ...), custom_call_target="tpu_custom_call" | custom-call | tf_op jit(solution)/shard_map/decode/pallas_call | solution.py:482
  216.4 0.0 copy-start.4
  216.4 2.1 copy-done.4
  218.5 0.0 copy-done.15
  218.6 0.2 fusion.1.src_ref
  218.8 2.3 %copy-done.5 = bf16[64,144,256]{2,1,0:T(8,128)(2,1)S(1)} copy-done((bf16[64,144,256]{2,1,0:T(8,128)(2,1)S(1)}, bf16[64,144,256]{2,1,0:T(8,128)(2,1)}, u32[]{:S(2)}) %copy-start.5) | copy-done | bytes 4718616
  221.1 8.1 %place_blocks.1 = bf16[32,64,576]{2,1,0:T(8,128)(2,1)} custom-call(s32[32]{0:T(128)S(1)} %fusion.1.src_ref, bf16[64,144,256]{2,1,0:T(8,128)(2,1)S(1)} %copy-done.5), custom_call_target="tpu_custom_call" | custom-call | tf_op jit(solution)/shard_map/place_blocks/pallas_call | solution.py:125
  229.2 0.0 copy-done.13
  229.2 0.9 convolution_convert_fusion
  230.1 0.6 copy.62
  230.7 0.6 copy.63
  (14 shorter events, 0.1 us)
Async XLA Ops:
  0.6 1.0 copy-start
  10.4 2.5 %copy-start.1 = (bf16[4,8,128,576]{3,2,1,0:T(8,128)(2,1)S(1)}, bf16[4,8,128,576]{3,2,1,0:T(8,128)(2,1)}, u32[]{:S(2)}) copy-start(bf16[4,8,128,576]{3,2,1,0:T(8,128)(2,1)} %copy.49.cache_ref) | copy-start | bytes 14155780
  12.9 24.3 %copy-start.19 = (s32[12]{0:T(128)S(1)}, s32[12]{0:T(128)}, u32[]{:S(2)}) copy-start(s32[12]{0:T(128)} %param.24) | copy-start | bytes 148
  32.5 2.1 copy-start.3
  34.6 1.5 copy-start.6
  39.4 3.9 %copy-start.14 = (bf16[512,32]{0,1:T(8,128)(2,1)S(1)}, bf16[512,32]{0,1:T(8,128)(2,1)}, u32[]{:S(2)}) copy-start(bf16[512,32]{0,1:T(8,128)(2,1)} %param.21) | copy-start | bytes 98308
  39.4 4.3 %copy-start.18 = (s32[4,8]{1,0:T(4,128)S(1)}, s32[4,8]{1,0:T(4,128)}, u32[]{:S(2)}) copy-start(s32[4,8]{1,0:T(4,128)} %param.23) | copy-start | bytes 388
  39.4 4.6 %copy-start.16 = (s32[12,6]{0,1:T(8,128)S(1)}, s32[12,6]{0,1:T(8,128)}, u32[]{:S(2)}) copy-start(s32[12,6]{0,1:T(8,128)} %param.30) | copy-start | bytes 868
  39.4 4.7 %copy-start.17 = (bf16[2048]{0:T(1024)(128)(2,1)S(1)}, bf16[2048]{0:T(1024)(128)(2,1)}, u32[]{:S(2)}) copy-start(bf16[2048]{0:T(1024)(128)(2,1)} %param.28) | copy-start | bytes 12292
  39.5 4.7 %copy-start.9 = (bf16[4,128,512]{2,1,0:T(8,128)(2,1)S(1)}, bf16[4,128,512]{2,1,0:T(8,128)(2,1)}, u32[]{:S(2)}) copy-start(bf16[4,128,512]{2,1,0:T(8,128)(2,1)} %key_hbm.1) | copy-start | bytes 1572868
  39.5 4.7 %copy-start.11 = (bf16[32,768]{1,0:T(8,128)(2,1)S(1)}, bf16[32,768]{1,0:T(8,128)(2,1)}, u32[]{:S(2)}) copy-start(bf16[32,768]{1,0:T(8,128)(2,1)} %qw_ref.1) | copy-start | bytes 147460
  39.5 4.7 %copy-start.12 = (bf16[12,32]{1,0:T(8,128)(2,1)S(1)}, bf16[12,32]{1,0:T(8,128)(2,1)}, u32[]{:S(2)}) copy-start(bf16[12,32]{1,0:T(8,128)(2,1)} %hidden_ref.1) | copy-start | bytes 2308
  44.2 1.4 copy-start.2
  45.6 1.7 copy-start.7
  47.3 1.4 copy-start.8
  48.7 1.0 copy-start.10
  49.8 168.8 %copy-start.15 = (s32[4,512]{1,0:T(4,128)S(1)}, s32[4,512]{1,0:T(4,128)}, u32[]{:S(2)}) copy-start(s32[4,512]{1,0:T(4,128)} %param.27) | copy-start | bytes 24580
  216.4 2.1 copy-start.4
  218.8 2.3 %copy-start.5 = (bf16[64,144,256]{2,1,0:T(8,128)(2,1)S(1)}, bf16[64,144,256]{2,1,0:T(8,128)(2,1)}, u32[]{:S(2)}) copy-start(bf16[64,144,256]{2,1,0:T(8,128)(2,1)} %copy-done.4) | copy-start | bytes 14155780
  221.1 8.1 %copy-start.13 = (bf16[4,512,64]{1,2,0:T(8,128)(2,1)S(1)}, bf16[4,512,64]{1,2,0:T(8,128)(2,1)}, u32[]{:S(2)}) copy-start(bf16[4,512,64]{1,2,0:T(8,128)(2,1)} %param.26) | copy-start | bytes 786436

commit v2 on v1

v2 whole, which is shorter than its diff:
```python
import functools

import jax
import jax.numpy as jnp
import numpy as np
from jax import lax
from jax.experimental import pallas as pl
from jax.experimental.pallas import tpu as pltpu
from jax.sharding import PartitionSpec as P

QK_NOPE = 128
QK_ROPE = 64
THETA = 50000.0
ROUTE_SCALE = 2.446
NORM_EPS = 1e-06
NEG = -1e30

MESH = pl.DeviceIdType.MESH
F32 = jnp.float32
BF16 = jnp.bfloat16

HERE = 4
PAGES = 8
BLOCKS = HERE * PAGES
ROWS = 128
KEPT = 64
RANK = 512
LATENT = 576
REQ = 12
GROUPS = 64
NX = 4
PACK = (144, 256)


def dot(a, b, dims=(((1,), (0,)), ((), ()))):
    return lax.dot_general(a, b, dims, preferred_element_type=F32)


NT = (((1,), (1,)), ((), ()))

OFFSETS = [
    (dy, sign * dz, dc)
    for dy in range(4)
    for dc in range(2)
    for dz in range(5)
    for sign in ((1,) if dz in (0, 4) else (1, -1))
    if (dy, dz, dc) != (0, 0, 0)
]
FEED = (0, 5, 5, 6, 5, 5, 5, 5, 5, 5, 5, 5, 5)


def split3(v):
    a = v.astype(BF16)
    rest = v - a.astype(F32)
    b = rest.astype(BF16)
    return a, b, (rest - b.astype(F32)).astype(BF16)


def lane_sum(v):
    total = v[:, 0:128]
    for n in range(1, v.shape[1] // 128):
        total = total + v[:, 128 * n : 128 * n + 128]
    for step in (64, 32, 16, 8, 4, 2, 1):
        total = total + pltpu.roll(total, step, 1)
    return total


def decode_kernel(
    seq_ref,
    table_ref,
    routes_ref,
    hidden_ref,
    qw_ref,
    place_ref,
    freq_ref,
    gain_ref,
    cache_hbm,
    keep_hbm,
    mass_hbm,
    key_hbm,
    value_hbm,
    out_hbm,
    router_hbm,
    gate_hbm,
    up_hbm,
    down_hbm,
    attn_ref,
    moe_ref,
    rows_ref,
    newmass_ref,
    pages,
    keep_v,
    mass_v,
    key_v,
    value_v,
    outw_v,
    router_v,
    gate_v,
    up_v,
    down_v,
    flat_v,
    packed,
    send_v,
    recv_v,
    index_v,
    index_s,
    q_out,
    q_in,
    q2_out,
    q2_in,
    q3_out,
    q3_in,
    a_out,
    a_in,
    b_out,
    b_in,
    c_out,
    c_in,
    d_out,
    d_in,
    d2_out,
    d2_in,
    d3_out,
    d3_in,
    e_out,
    e_in,
    e2_out,
    e2_in,
    e3_out,
    e3_in,
    e4_out,
    e4_in,
    load_sem,
    page_sem,
    index_sem,
    small_send,
    small_recv,
    bulk_send,
    bulk_recv,
):
    x = lax.axis_index("head")
    p = lax.axis_index("page")
    y, z, c = p // 16, (p // 2) % 8, p % 2
    a = y * 2 + c

    barrier = pltpu.get_barrier_semaphore()

    def greet(k, carry):
        pl.semaphore_signal(
            barrier, inc=1, device_id=(x, (p + k) % GROUPS), device_id_type=MESH
        )
        return carry

    lax.fori_loop(1, GROUPS, greet, 0)
    for k in range(1, NX):
        pl.semaphore_signal(barrier, inc=1, device_id=((x + k) % NX, p), device_id_type=MESH)

    keep_load = pltpu.make_async_copy(keep_hbm, keep_v, load_sem.at[0])
    keep_load.start()
    page_loads = [
        pltpu.make_async_copy(cache_hbm.at[h], pages.at[h], page_sem.at[h]) for h in range(HERE)
    ]
    for load in page_loads:
        load.start()
    loads = [
        pltpu.make_async_copy(src, dst, load_sem.at[n + 1])
        for n, (src, dst) in enumerate(
            (
                (key_hbm, key_v),
                (mass_hbm, mass_v),
                (value_hbm, value_v),
                (out_hbm, outw_v),
                (router_hbm, router_v),
                (gate_hbm.at[0], gate_v),
                (up_hbm.at[0], up_v),
                (down_hbm.at[0], down_v),
            )
        )
    ]
    for load in loads:
        load.start()

    lanes = GROUPS * PAGES
    for_device = jnp.zeros((GROUPS, lanes), jnp.int32)
    for_place = jnp.zeros((BLOCKS, lanes), jnp.int32)
    device = lax.broadcasted_iota(jnp.int32, (GROUPS, lanes), 0)
    place = lax.broadcasted_iota(jnp.int32, (BLOCKS, lanes), 0) + p * BLOCKS
    page = lax.broadcasted_iota(jnp.int32, (1, lanes), 1)
    for h in range(HERE):
        row = place_ref[h : h + 1, :]
        target = jnp.where(page // PAGES == p, row // BLOCKS, -1)
        for_device = jnp.where(target == device, h * PAGES + page % PAGES, for_device)
        for_place = jnp.where(row == place, page // PAGES, for_place)
    index_v[0:GROUPS] = jnp.minimum(lane_sum(for_device), BLOCKS - 1)
    index_v[GROUPS:] = jnp.minimum(lane_sum(for_place), GROUPS - 1)
    index_load = pltpu.make_async_copy(index_v, index_s, index_sem)
    index_load.start()

    part = dot(hidden_ref[...], qw_ref[...])
    width = QK_NOPE + QK_ROPE
    for h in range(HERE):
        q_out[h] = part[:, width * h : width * h + QK_NOPE]
    for n in range(2):
        q_out[HERE + n] = jnp.concatenate(
            [part[:, width * h + QK_NOPE : width * (h + 1)] for h in (2 * n, 2 * n + 1)],
            axis=1,
        )
    q_out[6] = jnp.zeros_like(q_out[6])
    q_out[7] = jnp.zeros_like(q_out[7])

    mine_pages = (
        lax.broadcasted_iota(jnp.int32, (PAGES, lanes), 1)
        == lax.broadcasted_iota(jnp.int32, (PAGES, lanes), 0) + p * PAGES
    )
    picker = mine_pages.astype(F32).astype(BF16)
    lane_row = lax.broadcasted_iota(jnp.int32, (KEPT, ROWS), 1).astype(F32)

    def compact(h):
        page_loads[h].wait()
        kept = dot(keep_v[h].astype(F32).astype(BF16), picker, NT)
        for g in range(PAGES):
            chosen = (kept[:, g : g + 1] == lane_row).astype(F32).astype(BF16)
            rows = dot(chosen, pages[h, g], NT)
            block = h * PAGES + g
            flat_v[h, KEPT * g : KEPT * g + KEPT, :] = rows.astype(BF16)
            packed[block, 0:64] = rows[:, 0:256].astype(BF16)
            packed[block, 64:128] = rows[:, 256:512].astype(BF16)
            rope = rows[:, 512:576]
            packed[block, 128:144] = jnp.concatenate(
                [rope[16 * n : 16 * n + 16] for n in range(4)], axis=1
            ).astype(BF16)

    keep_load.wait()
    compact(0)
    compact(1)
    index_load.wait()

    pl.semaphore_wait(barrier, GROUPS - 1 + NX - 1)

    fed = []

    def bulk(offset):
        dy, dz, dc = offset
        n = OFFSETS.index(offset)
        to = ((y + dy) % 4) * 16 + ((z + dz + 8) % 8) * 2 + (c + dc) % 2
        return to, pltpu.make_async_remote_copy(
            send_v.at[n],
            recv_v.at[p],
            bulk_send.at[n],
            bulk_recv.at[n],
            device_id=(x, to),
            device_id_type=MESH,
        )

    def feed(count):
        for offset in OFFSETS[len(fed) : len(fed) + count]:
            to, copy = bulk(offset)
            send_v[len(fed)] = packed[index_s[to, 0]]
            copy.start()
            fed.append(copy)

    smalls = []

    def exchange(stage, kind, out, into, scatter, meanwhile=None):
        copies = []
        size = NX if kind == "x" else 8
        me = {"a": a, "z": z, "x": x}[kind]
        for k in range(1, size):
            other = (me + k) % size
            if kind == "a":
                target = (x, (other // 2) * 16 + z * 2 + other % 2)
            elif kind == "z":
                target = (x, y * 16 + other * 2 + c)
            else:
                target = (other, p)
            copies.append(
                pltpu.make_async_remote_copy(
                    out.at[other] if scatter else out,
                    into.at[me],
                    small_send.at[stage, k],
                    small_recv.at[stage, k],
                    device_id=target,
                    device_id_type=MESH,
                )
            )
        for copy in copies:
            copy.start()
        into[me] = out[me] if scatter else out[...]
        if meanwhile is not None:
            meanwhile()
        feed(FEED[stage])
        for copy in copies:
            copy.wait_recv()
        smalls.extend(copies)

    def added(into, size):
        total = into[0].astype(F32)
        for n in range(1, size):
            total = total + into[n].astype(F32)
        return total

    def compact_rest():
        compact(2)
        compact(3)

    exchange(0, "a", q_out, q_in, True, compact_rest)
    recv_v[p] = packed[index_s[p, 0]]
    q2_out[...] = added(q_in, 8)
    exchange(1, "z", q2_out, q2_in, False)
    mine = added(q2_in, 8)
    request = lax.broadcasted_iota(jnp.int32, mine.shape, 0)
    lane = lax.broadcasted_iota(jnp.int32, mine.shape, 1)
    position = jnp.zeros(mine.shape, jnp.int32)
    for r in range(REQ):
        position = jnp.where(request == r, seq_ref[r] * ROWS - 1, position)
    angle = position.astype(F32) * freq_ref[...]
    first = lane % 64 < 32
    turned = jnp.where(first, -pltpu.roll(mine, 96, 1), pltpu.roll(mine, 32, 1))
    rotated = mine * jnp.cos(angle) + turned * jnp.sin(angle)
    q3_out[...] = jnp.where(a < HERE, mine, rotated).astype(BF16)
    exchange(2, "a", q3_out, q3_in, False)

    loads[0].wait()
    loads[1].wait()
    scale = width ** (-0.5)
    rows_here = PAGES * KEPT
    request = lax.broadcasted_iota(jnp.int32, (REQ, rows_here), 0)
    page = lax.broadcasted_iota(jnp.int32, (1, rows_here), 1) // KEPT
    ends = [seq_ref[0]]
    for r in range(1, REQ):
        ends.append(ends[-1] + seq_ref[r])

    def stats_of(best, total):
        return jnp.concatenate(
            [jnp.broadcast_to(v.astype(F32), (REQ, 16)) for v in (*split3(best), *split3(total))]
            + [jnp.zeros((REQ, 32), F32)],
            axis=1,
        ).astype(BF16)

    for h in range(HERE):
        logical = jnp.zeros((1, rows_here), jnp.int32)
        for g in range(PAGES):
            logical = jnp.where(page == g, table_ref[h, g], logical)
        owner = jnp.zeros((1, rows_here), jnp.int32)
        for r in range(REQ):
            owner = owner + (logical >= ends[r]).astype(jnp.int32)
        mass = dot(picker, mass_v[h], NT)
        mass = jnp.concatenate([mass[g : g + 1] for g in range(PAGES)], axis=1)
        rope = q3_in[HERE + h // 2][:, 64 * (h % 2) : 64 * (h % 2) + 64]
        latent_query = dot(q3_in[h], key_v[h]).astype(BF16)
        scores = dot(latent_query, flat_v[h, :, :RANK], NT) + dot(rope, flat_v[h, :, RANK:], NT)
        scores = scores * scale
        mine_here = owner == request
        best = jnp.max(jnp.where(mine_here, scores, NEG), axis=1, keepdims=True)
        weights = jnp.where(mine_here, mass * jnp.exp(scores - best), 0.0)
        total = jnp.sum(weights, axis=1, keepdims=True)
        summed = dot(weights.astype(BF16), flat_v[h, :, :RANK])
        stats = stats_of(best, total)
        for half in range(2):
            a_out[2 * h + half, :, 0:256] = summed[:, 256 * half : 256 * half + 256].astype(BF16)
            a_out[2 * h + half, :, 256:384] = stats

    def merged(into):
        def stat(n, first):
            return sum(
                into[n, :, 256 + 16 * s : 256 + 16 * s + 16].astype(F32)[:, 0:1]
                for s in range(first, first + 3)
            )

        bests = [stat(n, 0) for n in range(8)]
        best = functools.reduce(jnp.maximum, bests)
        total = jnp.zeros((REQ, 1), F32)
        latent = jnp.zeros((REQ, 256), F32)
        for n in range(8):
            factor = jnp.exp(bests[n] - best)
            total = total + factor * stat(n, 3)
            latent = latent + factor * into[n, :, 0:256].astype(F32)
        return best, total, latent

    exchange(3, "a", a_out, a_in, True)
    best, total, latent = merged(a_in)
    b_out[:, 0:256] = latent.astype(BF16)
    b_out[:, 256:384] = stats_of(best, total)
    exchange(4, "z", b_out, b_in, False)
    _, total, latent = merged(b_in)
    latent_out = (latent / total).astype(BF16)
    loads[2].wait()
    c_out[...] = dot(latent_out, value_v[a // 2, pl.ds((a % 2) * 256, 256), :])
    exchange(5, "a", c_out, c_in, False)

    loads[3].wait()
    cols = jnp.zeros((REQ, 32), F32)
    for h in range(HERE):
        head_out = (c_in[2 * h] + c_in[2 * h + 1]).astype(BF16)
        cols = cols + dot(head_out, outw_v[:, 128 * h : 128 * h + 128], NT)
    spread = jnp.concatenate([cols] * 4, axis=1)
    lane = lax.broadcasted_iota(jnp.int32, spread.shape, 1)
    d_out[...] = jnp.where(lane // 32 == p % 4, spread, 0.0)
    exchange(6, "x", d_out, d_in, False)
    d2_out[...] = added(d_in, NX).astype(BF16)
    exchange(7, "z", d2_out, d2_in, False)
    for n in range(4):
        d3_out[n] = (d2_in[2 * n].astype(F32) + d2_in[2 * n + 1].astype(F32)).astype(BF16)
    exchange(8, "a", d3_out, d3_in, False)

    tiles = [
        d3_in[2 * (t // 4), t % 4].astype(F32) + d3_in[2 * (t // 4) + 1, t % 4].astype(F32)
        for t in range(16)
    ]
    square = jnp.zeros((REQ, 128), F32)
    for t in range(16):
        attn_ref[:, 128 * t : 128 * t + 128] = tiles[t].astype(BF16)
        square = square + tiles[t] * tiles[t]
    mean = jnp.sum(square, axis=1, keepdims=True) * (1.0 / 2048)
    inverse = lax.rsqrt(mean + NORM_EPS)
    normed = jnp.concatenate(
        [
            (tiles[t] * inverse * gain_ref[:, 128 * t : 128 * t + 128].astype(F32)).astype(BF16)
            for t in range(16)
        ],
        axis=1,
    )

    loads[4].wait()
    logits = dot(normed, router_v[...], NT)
    chance = 1.0 / (1.0 + jnp.exp(-logits))
    expert = lax.broadcasted_iota(jnp.int32, chance.shape, 1)
    request = lax.broadcasted_iota(jnp.int32, chance.shape, 0)
    routed = jnp.zeros(chance.shape, F32)
    for t in range(routes_ref.shape[0]):
        route = jnp.zeros(chance.shape, jnp.int32)
        for r in range(REQ):
            route = jnp.where(request == r, routes_ref[t, r], route)
        routed = jnp.where(route == expert, 1.0, routed)
    chosen = routed * chance
    share = ROUTE_SCALE * chosen / jnp.sum(chosen, axis=1, keepdims=True)
    share_here = jnp.sum(jnp.where(expert == p, share, 0.0), axis=1, keepdims=True)
    loads[5].wait()
    gate = dot(normed, gate_v[...], NT)
    loads[6].wait()
    up = dot(normed, up_v[...], NT)
    expert_hidden = (gate / (1.0 + jnp.exp(-gate)) * up).astype(BF16)
    loads[7].wait()
    for n in range(8):
        e_out[n] = (
            share_here * dot(expert_hidden, down_v[:, 256 * n : 256 * n + 256])
        ).astype(BF16)
    exchange(9, "a", e_out, e_in, True)
    e2_out[...] = added(e_in, 8).astype(BF16)
    exchange(10, "z", e2_out, e2_in, False)
    e3_out[...] = added(e2_in, 8).astype(BF16)
    exchange(11, "x", e3_out, e3_in, False)
    e4_out[...] = added(e3_in, NX).astype(BF16)
    exchange(12, "a", e4_out, e4_in, False)
    feed(len(OFFSETS))
    for n in range(8):
        moe_ref[:, 256 * n : 256 * n + 256] = e4_in[n]

    place = lax.broadcasted_iota(jnp.int32, (BLOCKS, lanes), 0) + p * BLOCKS
    new_mass = jnp.zeros((BLOCKS, KEPT), F32)
    for h in range(HERE):
        owned = (place_ref[h : h + 1, :] == place).astype(F32).astype(BF16)
        new_mass = new_mass + dot(owned, mass_v[h], NT)
    newmass_ref[...] = new_mass.astype(BF16)

    for copy in smalls:
        copy.wait_send()
    for copy in fed:
        copy.wait()

    def put(q, carry):
        block = recv_v[index_s[GROUPS + q, 0]]
        rows_ref[q, :, 0:256] = block[0:64]
        rows_ref[q, :, 256:512] = block[64:128]
        rope = block[128:144].astype(F32)
        rows_ref[q, :, 512:576] = jnp.concatenate(
            [rope[:, 64 * n : 64 * n + 64] for n in range(4)], axis=0
        ).astype(BF16)
        return carry

    lax.fori_loop(0, BLOCKS, put, 0)


def decode(*operands):
    smem = [pl.BlockSpec(memory_space=pltpu.SMEM)] * 3
    small = [pl.BlockSpec(memory_space=pltpu.VMEM)] * 5
    big = [pl.BlockSpec(memory_space=pltpu.HBM)] * 10
    tile = (REQ, 128)
    wide = (REQ, 256)
    stat = (REQ, 384)

    def pair(shape, parts, dtype, scatter):
        return [
            pltpu.VMEM((parts, *shape) if scatter else shape, dtype),
            pltpu.VMEM((parts, *shape), dtype),
        ]

    return pl.pallas_call(
        decode_kernel,
        out_shape=(
            jax.ShapeDtypeStruct((REQ, 2048), BF16),
            jax.ShapeDtypeStruct((REQ, 2048), BF16),
            jax.ShapeDtypeStruct((BLOCKS, KEPT, LATENT), BF16),
            jax.ShapeDtypeStruct((BLOCKS, KEPT), BF16),
        ),
        in_specs=smem + small + big,
        out_specs=(pl.BlockSpec(memory_space=pltpu.VMEM),) * 4,
        scratch_shapes=[
            pltpu.VMEM((HERE, PAGES, LATENT, ROWS), BF16),
            pltpu.VMEM((HERE, KEPT, GROUPS * PAGES), jnp.int32),
            pltpu.VMEM((HERE, KEPT, GROUPS * PAGES), BF16),
            pltpu.VMEM((HERE, QK_NOPE, RANK), BF16),
            pltpu.VMEM((HERE, RANK, 128), BF16),
            pltpu.VMEM((32, 512), BF16),
            pltpu.VMEM((64, 2048), BF16),
            pltpu.VMEM((352, 2048), BF16),
            pltpu.VMEM((352, 2048), BF16),
            pltpu.VMEM((352, 2048), BF16),
            pltpu.VMEM((HERE, PAGES * KEPT, LATENT), BF16),
            pltpu.VMEM((BLOCKS, *PACK), BF16),
            pltpu.VMEM((GROUPS - 1, *PACK), BF16),
            pltpu.VMEM((GROUPS, *PACK), BF16),
            pltpu.VMEM((GROUPS + BLOCKS, 128), jnp.int32),
            pltpu.SMEM((GROUPS + BLOCKS, 128), jnp.int32),
            *pair(tile, 8, F32, True),
            *pair(tile, 8, F32, False),
            *pair(tile, 8, BF16, False),
            *pair(stat, 8, BF16, True),
            *pair(stat, 8, BF16, False),
            *pair(tile, 8, F32, False),
            *pair(tile, NX, F32, False),
            *pair(tile, 8, BF16, False),
            *pair((4, *tile), 8, BF16, False),
            *pair(wide, 8, BF16, True),
            *pair(wide, 8, BF16, False),
            *pair(wide, NX, BF16, False),
            *pair(wide, 8, BF16, False),
            pltpu.SemaphoreType.DMA((9,)),
            pltpu.SemaphoreType.DMA((HERE,)),
            pltpu.SemaphoreType.DMA,
            pltpu.SemaphoreType.DMA((13, 8)),
            pltpu.SemaphoreType.DMA((13, 8)),
            pltpu.SemaphoreType.DMA((GROUPS,)),
            pltpu.SemaphoreType.DMA((GROUPS,)),
        ],
        compiler_params=pltpu.CompilerParams(
            collective_id=0, has_side_effects=True, vmem_limit_bytes=56 << 20
        ),
        name="decode",
    )(*operands)


def shards(
    hidden,
    q_weight,
    key_up,
    value_up_weight,
    out_weight,
    cache,
    page_table,
    seq_pages,
    keep_rows,
    fold_mass,
    new_place,
    norm_gain,
    router,
    routes,
    w_gate,
    w_up,
    w_down,
):
    half = QK_ROPE // 2
    freqs = THETA ** (-2.0 * np.arange(half) / QK_ROPE)
    freqs = jnp.asarray(np.tile(freqs, 4)[None, :], F32)

    def turn(array):
        return jnp.swapaxes(array, -1, -2)

    return decode(
        seq_pages,
        page_table,
        turn(routes),
        hidden,
        q_weight,
        new_place,
        freqs,
        norm_gain.reshape(1, -1),
        turn(cache),
        turn(keep_rows),
        turn(fold_mass),
        key_up,
        value_up_weight,
        turn(out_weight),
        turn(router),
        turn(w_gate),
        turn(w_up),
        w_down,
    )


def solution(mesh):
    in_specs = (
        P(None, "page"),
        P("page", "head"),
        P("head", None, None),
        P("head", None, None),
        P("head", "page"),
        P("head", "page", None, None),
        P("head", "page"),
        P(),
        P("head", None, None),
        P("head", None, None),
        P("head", None),
        P(),
        P(),
        P(),
        P("page", None, "head"),
        P("page", None, "head"),
        P("page", "head", None),
    )
    out_specs = (P(), P(), P(("head", "page"), None, None), P(("head", "page"), None))
    return jax.shard_map(shards, mesh=mesh, in_specs=in_specs, out_specs=out_specs, check_vma=False)
```

time: 232 us -> 150 us (0.65)
  the two profiles are of different devices: /device:TPU:123 before, /device:TPU:1 now
where the time goes in v2:
time: 150 us; the launch traced here: 147 us
  Pallas kernels  138 us (92%)
  local copies, waits for them, and re-layouts  8.31 us (6%)
    pallas_call x1, Pallas kernels, decode(): pl.pallas_call(decode_kernel, out_shape=(jax.ShapeDtypeStruct((REQ, 2048)...  138 us
    unnamed x6, local copies, waits for them, and re-layouts  7.02 us

profile of v2, /device:TPU:1, one launch (start us, length us, event | category | flops | bytes accessed | tf_op | source)
XLA Modules:
  0.0 147.0 jit_solution(6216369661076670902)
XLA Ops:
  0.6 1.3 reshape.11.gain_ref
  1.9 138.0 %decode.1 = (bf16[12,2048]{1,0:T(8,128)(2,1)}, bf16[12,2048]{1,0:T(8,128)(2,1)}, bf16[32,64,576]{2,1,0:T(8,128)(2,1)}, bf16[32,64]{1,0:T(8,128)(2,1)}) custom-call(s32[12]{0:T(128)} %seq_ref.1, s32[4,8]{1,0:T(4,128)} %table_ref.1, s32[6,12]{1,0:T(8,128)} %bitcast.15, bf16[12,32]{1,0:T(8,128)(2,1)} %hidden_ref.1, bf16[32,768]{1,0:T(8,128)(2,1)} %qw_ref.1, ...), custom_call_target="tpu_custom_call" | custom-call | tf_op jit(solution)/shard_map/decode/pallas_call | solution.py:498
  139.9 1.5 %copy.26 = bf16[12,2048]{1,0:T(8,128)(2,1)} copy(bf16[12,2048]{1,0:T(8,128)(2,1)} %get-tuple-element.8) | data formatting | bytes 98304
  141.4 1.5 %copy.27 = bf16[12,2048]{1,0:T(8,128)(2,1)} copy(bf16[12,2048]{1,0:T(8,128)(2,1)} %get-tuple-element.9) | data formatting | bytes 98304
  142.9 0.0 copy-start
  142.9 3.5 %copy.28 = bf16[32,64,576]{2,1,0:T(8,128)(2,1)} copy(bf16[32,64,576]{2,1,0:T(8,128)(2,1)} %get-tuple-element.10) | data formatting | bytes 4718592
  146.4 0.0 copy-done
  146.4 0.6 copy.29
Async XLA Ops:
  142.9 3.5 %copy-start = (bf16[32,64]{1,0:T(8,128)(2,1)S(1)}, bf16[32,64]{1,0:T(8,128)(2,1)}, u32[]{:S(2)}) copy-start(bf16[32,64]{1,0:T(8,128)(2,1)} %get-tuple-element.11) | copy-start | bytes 12292
